TPU v7x, 32 devices: a whole 2x2x4 slice. The times are simulated.
32 devices in a mesh: fsdp: 8 (over z, x), side: 4 (over y, core).
Axes of the slice: x: 2, y: 2, z: 4, core: 2. Of those that a mesh axis runs over, the one named last changes fastest.
Arguments:
- attn_inputs: bfloat16 [4096, 5120], P(('side', 'fsdp')), may hold values from -6 to 6
- queries: bfloat16 [4096, 2560], P(('side', 'fsdp')), may hold values from -310 to 310
- key_vectors: bfloat16 [4096, 512], P(('side', 'fsdp')), may hold values from -12 to 12
- logp_grad: bfloat16 [4096, 2560], P(('side', 'fsdp')), may hold values from -24 to 24
- new_logp: float32 [4096], P(('side', 'fsdp')), may hold values from -6.5 to -0.01
- old_logp: float32 [4096], P(('side', 'fsdp')), may hold values from -4 to -0.05
- rewards: float32 [8], replicated, may hold values from -8 to 8
- group_ids: int32 [8], replicated, may hold values from 0 to 1
- lengths: int32 [8], replicated, may hold values from 256 to 512
- value_proj: bfloat16 [5120, 512], P('fsdp'), may hold values from -0.078125 to 0.078125
- first_moment: bfloat16 [5120, 512], P(('fsdp', 'side')), may hold values from -120 to 120
- second_moment: bfloat16 [5120, 512], P(('fsdp', 'side')), may hold values from 100 to 9984
Outputs:
- input_grad: bfloat16 [4096, 5120], P(('side', 'fsdp'))
- new_proj: bfloat16 [5120, 512], P('fsdp')
- new_first: bfloat16 [5120, 512], P(('fsdp', 'side'))
- new_second: bfloat16 [5120, 512], P(('fsdp', 'side'))
All inputs are finite; a program needn't handle non-finite values.
Results may differ from a plain program's by a relative error of at most 0.03.
Values may be sent and summed in bfloat16 or wider, within the bound.
No kernel may reach another device: no remote copies, remote signals or barrier semaphores. Data moves between devices by JAX's collectives and lax.ppermute only.
A program may use at most 64 MiB of HBM per device.

v0:
```python
import math
import jax
import jax.numpy as jnp
from jax import lax
from jax.sharding import PartitionSpec as P

QH = 20
KVH = 4
HEAD = 128
ROLLS = 2
clip_low = 0.8
clip_high = 1.2
decay_first = 0.9
decay_second = 0.95
step_rate = 0.001
weight_decay = 0.1
adam_eps = 1e-08
bias_first = 1.0 - 0.9**10
bias_second = 1.0 - 0.95**10


def advantages(rewards, group_ids):
    group_count = rewards.shape[0] // 4
    member = (group_ids[:, None] == jnp.arange(group_count, dtype=jnp.int32)[None, :]).astype(
        jnp.float32
    )
    counts = jnp.maximum(jnp.sum(member, axis=0), 1.0)
    group_mean = jnp.sum(member * rewards[:, None], axis=0) / counts
    own_mean = jnp.sum(member * group_mean[None, :], axis=1)
    spread = rewards - own_mean
    variance = jnp.sum(member * (spread * spread)[:, None], axis=0) / counts
    own_std = jnp.sqrt(jnp.sum(member * variance[None, :], axis=1))
    return spread / jnp.maximum(own_std, 1.0)


def coefficient(new_lp, old_lp, adv_tok, len_tok, pos_tok, full_len):
    ratio_now = jnp.exp(new_lp - old_lp)
    clipped = jnp.clip(ratio_now, clip_low, clip_high)
    active = (ratio_now * adv_tok <= clipped * adv_tok) & (pos_tok < len_tok)
    len_weight = full_len / len_tok.astype(jnp.float32)
    return jnp.where(active, -adv_tok * ratio_now * len_weight, 0.0)


def block_values(query_blk, grad_blk, roll_keys, first_pos):
    tok_rows = query_blk.shape[0]
    key_count = roll_keys.shape[0]
    per_group = QH // KVH
    score_scale = 1.0 / math.sqrt(HEAD)
    query_pos = first_pos + jnp.arange(tok_rows, dtype=jnp.int32)
    key_pos = jnp.arange(key_count, dtype=jnp.int32)
    allowed = jnp.tile(key_pos[None, :] <= query_pos[:, None], (per_group, 1))
    pieces = []
    for kv_head in range(KVH):
        col_low = kv_head * per_group * HEAD
        col_high = col_low + per_group * HEAD
        q_part = (
            query_blk[:, col_low:col_high]
            .reshape(tok_rows, per_group, HEAD)
            .transpose(1, 0, 2)
            .reshape(per_group * tok_rows, HEAD)
        )
        g_part = (
            grad_blk[:, col_low:col_high]
            .reshape(tok_rows, per_group, HEAD)
            .transpose(1, 0, 2)
            .reshape(per_group * tok_rows, HEAD)
        )
        k_part = roll_keys[:, kv_head * HEAD : (kv_head + 1) * HEAD]
        scores = jnp.dot(q_part, k_part.T, preferred_element_type=jnp.float32) * score_scale
        scores = jnp.where(allowed, scores, -1e30)
        top_val = jnp.max(scores, axis=1, keepdims=True)
        expo = jnp.exp(scores - top_val)
        attention = (expo / jnp.sum(expo, axis=1, keepdims=True)).astype(jnp.bfloat16)
        pieces.append(jnp.dot(attention.T, g_part, preferred_element_type=jnp.float32))
    return jnp.concatenate(pieces, axis=1)


def adam_rows(old_rows, grad_rows, first_moment, second_moment):
    first = decay_first * first_moment.astype(jnp.float32) + (1.0 - decay_first) * grad_rows
    second = (
        decay_second * second_moment.astype(jnp.float32)
        + (1.0 - decay_second) * grad_rows * grad_rows
    )
    weight_now = old_rows.astype(jnp.float32)
    update = (
        first / bias_first / (jnp.sqrt(second / bias_second) + adam_eps) + weight_decay * weight_now
    )
    return (
        (weight_now - step_rate * update).astype(jnp.bfloat16),
        first.astype(jnp.bfloat16),
        second.astype(jnp.bfloat16),
    )


def shards(
    attn_inputs,
    queries,
    key_vectors,
    logp_grad,
    new_logp,
    old_logp,
    rewards,
    group_ids,
    lengths,
    value_proj,
    first_moment,
    second_moment,
):
    fsdp_size = lax.axis_size("fsdp")
    fsdp_index = lax.axis_index("fsdp")
    side_index = lax.axis_index("side")
    tok_rows = attn_inputs.shape[0]
    half = tok_rows // ROLLS
    full_len = half * fsdp_size
    width = key_vectors.shape[1]
    first_pos = fsdp_index * half
    advantage = advantages(rewards, group_ids)
    slot = jnp.arange(tok_rows, dtype=jnp.int32)
    global_roll = side_index * ROLLS + slot // half
    position = first_pos + slot % half
    coeff = coefficient(
        new_logp, old_logp, advantage[global_roll], lengths[global_roll], position, full_len
    )
    out_grad = (coeff[:, None] * logp_grad.astype(jnp.float32)).astype(jnp.bfloat16)
    in_columns = lax.all_to_all(attn_inputs, "fsdp", split_axis=1, concat_axis=0, tiled=True)
    all_keys = lax.all_gather(key_vectors, "fsdp", axis=0, tiled=True)
    keys_split = all_keys.reshape(fsdp_size, ROLLS, half, width)
    partials = []
    for roll in range(ROLLS):
        roll_keys = keys_split[:, roll].reshape(full_len, width)
        partials.append(
            block_values(
                queries[roll * half : (roll + 1) * half],
                out_grad[roll * half : (roll + 1) * half],
                roll_keys,
                first_pos,
            )
        )
    stacked = jnp.stack(partials, axis=0)
    placed = (
        stacked.reshape(ROLLS, fsdp_size, half, width)
        .transpose(1, 0, 2, 3)
        .reshape(fsdp_size * tok_rows, width)
    )
    values_grad = lax.psum(placed.astype(jnp.bfloat16), "fsdp")
    grad_cols = jnp.dot(values_grad, value_proj.T, preferred_element_type=jnp.float32).astype(
        jnp.bfloat16
    )
    input_grad = lax.all_to_all(grad_cols, "fsdp", split_axis=0, concat_axis=1, tiled=True)
    weight_grad = lax.dot_general(
        in_columns, values_grad, (((0,), (0,)), ((), ())), preferred_element_type=jnp.float32
    )
    shard_grad = lax.psum_scatter(
        weight_grad.astype(jnp.bfloat16), "side", scatter_dimension=0, tiled=True
    ).astype(jnp.float32)
    shard_rows = shard_grad.shape[0]
    old_rows = lax.dynamic_slice_in_dim(value_proj, side_index * shard_rows, shard_rows, 0)
    new_rows, new_first, new_second = adam_rows(old_rows, shard_grad, first_moment, second_moment)
    new_proj = lax.all_gather(new_rows, "side", axis=0, tiled=True)
    return (input_grad, new_proj, new_first, new_second)


def solution(mesh):
    placed = (
        P(("side", "fsdp"), None),
        P(("side", "fsdp"), None),
        P(("side", "fsdp"), None),
        P(("side", "fsdp"), None),
        P(("side", "fsdp")),
        P(("side", "fsdp")),
        P(),
        P(),
        P(),
        P("fsdp", None),
        P(("fsdp", "side"), None),
        P(("fsdp", "side"), None),
    )
    return jax.shard_map(
        shards,
        mesh=mesh,
        in_specs=placed,
        out_specs=(
            P(("side", "fsdp"), None),
            P("fsdp", None),
            P(("fsdp", "side"), None),
            P(("fsdp", "side"), None),
        ),
        check_vma=False,
    )
```

profile of v0, /device:TPU:0, one launch (start us, length us, event | category | flops | bytes accessed | tf_op | source)
XLA Modules:
  0.0 208.1 jit_solution(15375847009809611103)
XLA Ops:
  7.2 0.7 all-gather.2.cloned.1.call-update
  7.9 2.4 %copy.153 = bf16[128,5120]{0,1:T(8,128)(2,1)} copy(bf16[128,5120]{1,0:T(8,128)(2,1)} %param.12) | data formatting | bytes 2621440 | tf_op args[0]
  10.4 7.4 %all-to-all-start.1 = ((bf16[128,8,640]{0,2,1:T(8,128)(2,1)}), bf16[128,8,640]{0,2,1:T(8,128)(2,1)S(1)}, u32[]{:S(2)}, u32[]{:S(2)}) async-start(bf16[128,8,640]{0,2,1:T(8,128)(2,1)} %bitcast.61), calls=%async_computation.1 | async-start | bytes 2621440 | tf_op jit(solution)/shard_map/all_to_all | solution.py:125
  18.4 0.7 fusion.40
  19.1 0.7 fusion.41
  19.7 10.1 %and_select_fusion = f32[128]{0:T(128)S(1)} fusion(f32[128]{0:T(128)S(1)} %copy-done.10, f32[128]{0:T(128)S(1)} %copy-done.11, s32[]{:T(128)} %bitcast.16, f32[]{:T(128)} %bitcast.7, s32[]{:T(128)} %bitcast.17, f32[]{:T(128)} %bitcast.8, s32[]{:T(128)} %bitcast.18, f32[]{:T(128)} %bitcast.9, s32[]{:T(128)} %bitcast.19, f32[]{:T(128)} %bitcast.10, ...), kind=kLoop, calls=%fused_computation.78 | loop fusion | flops 6784 | bytes 1608 | tf_op jit(solution)/shard_map/jit(_where)/select_n | solution.py:41
  30.3 0.7 copy-done.2
  32.9 0.6 copy.149
  33.8 28.8 %all-gather.2.cloned.1.call-done = bf16[1024,512]{1,0:T(8,128)(2,1)} async-done(((bf16[128,512]{1,0:T(8,128)(2,1)}), bf16[1024,512]{1,0:T(8,128)(2,1)}) %all-gather.2.cloned.1.call-update) | async-done | bytes 1048592 | tf_op jit(solution)/shard_map/all_gather | solution.py:126
  62.7 1.3 fusion.37
  64.0 0.4 fusion.48
  64.4 0.4 fusion.49
  64.7 0.4 fusion.47
  65.1 0.4 fusion.46
  65.4 0.4 fusion.45
  65.8 0.4 fusion.44
  66.2 0.4 fusion.43
  66.5 0.4 fusion.42
  66.9 0.3 fusion.10
  67.2 0.4 convolution_convert_fusion.8
  67.5 0.3 fusion.9
  67.8 0.4 convolution_convert_fusion.9
  68.2 0.3 fusion.11
  68.5 0.4 convolution_convert_fusion.7
  68.8 0.3 fusion.12
  69.1 0.4 convolution_convert_fusion.6
  69.5 0.3 fusion.13
  69.8 0.4 convolution_convert_fusion.5
  70.1 0.3 fusion.14
  70.4 0.4 convolution_convert_fusion.4
  70.8 0.3 fusion.15
  71.1 1.0 copy.141
  72.4 0.4 convolution_convert_fusion.3
  72.7 0.5 copy-done.5
  73.3 0.4 convolution_convert_fusion.2
  73.9 0.8 copy-done
  74.8 1.1 copy.151
  75.9 77.6 %all-reduce.2.cloned.1.call-done = bf16[1024,512]{1,0:T(8,128)(2,1)} async-done(((bf16[1024,512]{1,0:T(8,128)(2,1)}), bf16[1024,512]{1,0:T(8,128)(2,1)}) %all-reduce.2.cloned.1.call-update) | async-done | bytes 1048592 | tf_op jit(solution)/shard_map/psum | solution.py:145
  153.5 3.3 %convolution_convert_fusion = bf16[1024,640]{1,0:T(8,128)(2,1)} fusion(bf16[1024,512]{1,0:T(8,128)(2,1)} %all-reduce.2.cloned.1.call-done, bf16[640,512]{1,0:T(8,128)(2,1)S(1)} %copy-done.6), kind=kOutput, calls=%fused_computation | convolution fusion | flops 671744000 | bytes 3014656 | tf_op jit(solution)/shard_map/dot_general | solution.py:146
  156.8 4.2 %all-to-all-start = ((bf16[8,128,640]{2,1,0:T(8,128)(2,1)}), bf16[8,128,640]{2,1,0:T(8,128)(2,1)S(1)}, u32[]{:S(2)}, u32[]{:S(2)}) async-start(bf16[8,128,640]{2,1,0:T(8,128)(2,1)} %bitcast.127), calls=%async_computation | async-start | bytes 2621440 | tf_op jit(solution)/shard_map/all_to_all | solution.py:149
  161.0 1.5 copy.154
  162.5 2.7 %fusion = bf16[640,512]{0,1:T(8,128)(2,1)S(1)} fusion(bf16[1024,512]{1,0:T(8,128)(2,1)} %all-reduce.2.cloned.1.call-done, bf16[1024,640]{1,0:T(8,128)(2,1)} %bitcast.129), kind=kOutput, calls=%fused_computation.3 | convolution fusion | flops 671416320 | bytes 3014656 | tf_op jit(solution)/shard_map/dot_general | solution.py:150
  165.2 1.1 copy.156
  166.3 23.9 %reduce-scatter.4.cloned.1.call-done = bf16[160,512]{1,0:T(8,128)(2,1)} async-done(((bf16[640,512]{1,0:T(8,128)(2,1)}), bf16[160,512]{1,0:T(8,128)(2,1)}) %reduce-scatter.4.cloned.1.call-update) | async-done | bytes 163856 | tf_op jit(solution)/shard_map/reduce_scatter | solution.py:153
  190.2 1.9 fusion.23
  192.2 7.3 %all_gather.7 = bf16[640,512]{1,0:T(8,128)(2,1)S(1)} all-gather(bf16[160,512]{1,0:T(8,128)(2,1)S(1)} %get-tuple-element.47), channel_id=1, replica_groups=mesh['fsdp'=8,'side'=4] {'side'}, dimensions={0}, use_global_device_ids=true | all-gather | bytes 819200 | tf_op jit(solution)/shard_map/all_gather | solution.py:159
  199.5 1.2 copy.158
  200.7 0.8 copy.169
  (78 shorter events, 3.7 us)
Async XLA Ops:
  7.2 55.5 %all-gather.2.cloned.1.call-start = ((), (), s32[]{:S(2)}) async-start(), calls=%async_computation.3 | async-start | bytes 1179648 | tf_op jit(solution)/shard_map/all_gather | solution.py:126
  10.3 7.5 %copy-start.8 = (f32[8]{0:T(128)S(1)}, f32[8]{0:T(128)}, u32[]{:S(2)}) copy-start(f32[8]{0:T(128)} %param.18) | copy-start | bytes 100
  10.3 7.5 %copy-start.9 = (s32[8]{0:T(128)S(1)}, s32[8]{0:T(128)}, u32[]{:S(2)}) copy-start(s32[8]{0:T(128)} %param.19) | copy-start | bytes 100
  10.3 8.7 %copy-start.7 = (s32[8]{0:T(128)S(1)}, s32[8]{0:T(128)}, u32[]{:S(2)}) copy-start(s32[8]{0:T(128)} %param.20) | copy-start | bytes 100
  10.3 9.4 %copy-start.10 = (f32[128]{0:T(128)S(1)}, f32[128]{0:T(128)}, u32[]{:S(2)}) copy-start(f32[128]{0:T(128)} %param.16) | copy-start | bytes 1540
  10.4 9.4 %copy-start.11 = (f32[128]{0:T(128)S(1)}, f32[128]{0:T(128)}, u32[]{:S(2)}) copy-start(f32[128]{0:T(128)} %param.17) | copy-start | bytes 1540
  10.4 19.5 %copy-start.1 = (bf16[128,2560]{1,0:T(8,128)(2,1)S(1)}, bf16[128,2560]{1,0:T(8,128)(2,1)}, u32[]{:S(2)}) copy-start(bf16[128,2560]{1,0:T(8,128)(2,1)} %param.15) | copy-start | bytes 1966084
  10.4 146.4 %all-to-all-start.1 = ((bf16[128,8,640]{0,2,1:T(8,128)(2,1)}), bf16[128,8,640]{0,2,1:T(8,128)(2,1)S(1)}, u32[]{:S(2)}, u32[]{:S(2)}) async-start(bf16[128,8,640]{0,2,1:T(8,128)(2,1)} %bitcast.61), calls=%async_computation.1 | async-start | bytes 2621440 | tf_op jit(solution)/shard_map/all_to_all | solution.py:125
  17.8 135.7 %all-reduce.2.cloned.1.call-start = ((), (), s32[]{:S(2)}) async-start(), calls=%async_computation.4 | async-start | bytes 2097152 | tf_op jit(solution)/shard_map/psum | solution.py:145
  29.8 1.1 copy-start.2
  72.4 0.9 copy-start.5
  73.6 1.0 copy-start
  74.8 78.7 %copy-start.6 = (bf16[640,512]{1,0:T(8,128)(2,1)S(1)}, bf16[640,512]{1,0:T(8,128)(2,1)}, u32[]{:S(2)}) copy-start(bf16[640,512]{1,0:T(8,128)(2,1)} %param.21) | copy-start | bytes 1966084
  156.8 42.7 %all-to-all-start = ((bf16[8,128,640]{2,1,0:T(8,128)(2,1)}), bf16[8,128,640]{2,1,0:T(8,128)(2,1)S(1)}, u32[]{:S(2)}, u32[]{:S(2)}) async-start(bf16[8,128,640]{2,1,0:T(8,128)(2,1)} %bitcast.127), calls=%async_computation | async-start | bytes 2621440 | tf_op jit(solution)/shard_map/all_to_all | solution.py:149
  161.0 29.2 %reduce-scatter.4.cloned.1.call-start = ((), (), s32[]{:S(2)}) async-start(), calls=%async_computation.5 | async-start | bytes 819200 | tf_op jit(solution)/shard_map/reduce_scatter | solution.py:153
  165.2 25.1 %copy-start.3 = (bf16[160,512]{1,0:T(8,128)(2,1)S(1)}, bf16[160,512]{1,0:T(8,128)(2,1)}, u32[]{:S(2)}) copy-start(bf16[160,512]{1,0:T(8,128)(2,1)} %param.23) | copy-start | bytes 491524
  165.2 25.1 %copy-start.4 = (bf16[160,512]{1,0:T(8,128)(2,1)S(1)}, bf16[160,512]{1,0:T(8,128)(2,1)}, u32[]{:S(2)}) copy-start(bf16[160,512]{1,0:T(8,128)(2,1)} %param.22) | copy-start | bytes 491524
Sparse Core Ops, SparseCore 0:
  10.1 52.5 all-gather.1
  76.0 77.4 all-reduce.1
  166.4 23.7 reduce-scatter.3
where the time goes:
time: 209 us; the launch traced here: 208 us
  waiting for transfers between devices  131 us (63%)
  local copies, waits for them, and re-layouts  16.8 us (8%)
  other arithmetic  15.1 us (7%)
  between operations  14.2 us (7%)
  matrix products  11.8 us (6%)
  starting transfers between devices  11.7 us (6%)
  blocking collectives  7.31 us (3%)
    psum x1, waiting for transfers between devices, shards(): values_grad = lax.psum(placed.astype(jnp.bfloat16), 'fsdp')  77.6 us
    all_gather x1, waiting for transfers between devices, shards(): all_keys = lax.all_gather(key_vectors, 'fsdp', axis=0, tiled=True)  28.8 us
    reduce_scatter x1, waiting for transfers between devices, shards(): lax.psum_scatter(weight_grad.astype(jnp.bfloat16), 'side', scatter_dimens...  23.9 us
    select_n x1, other arithmetic, coefficient(): return jnp.where(active, -adv_tok * ratio_now * len_weight, 0.0)  10.1 us
    all_to_all x1, starting transfers between devices, shards(): lax.all_to_all(attn_inputs, 'fsdp', split_axis=1, concat_axis=0, tiled=True)  7.42 us
    all_gather x1, blocking collectives, shards(): new_proj = lax.all_gather(new_rows, 'side', axis=0, tiled=True)  7.31 us
    unnamed x27, local copies, waits for them, and re-layouts  6.41 us
    all_to_all x1, starting transfers between devices, shards(): lax.all_to_all(grad_cols, 'fsdp', split_axis=0, concat_axis=1, tiled=True)  4.21 us
  transfers between devices with their start and end apart: 5, of which 3 were waited for; matrix products, arithmetic and copies ran while one was open for 19% of the time, Pallas kernels for 0%

commit v1 on v0

--- a/solution.py
+++ b/solution.py
@@ -142,7 +142,7 @@
         .transpose(1, 0, 2, 3)
         .reshape(fsdp_size * tok_rows, width)
     )
-    values_grad = lax.psum(placed.astype(jnp.bfloat16), "fsdp")
+    values_grad = jnp.sum(lax.all_gather(placed.astype(jnp.bfloat16), "fsdp"), axis=0)
     grad_cols = jnp.dot(values_grad, value_proj.T, preferred_element_type=jnp.float32).astype(
         jnp.bfloat16
     )

time: 209 us -> 271 us (1.30)
  waiting for transfers between devices: 131 us -> 191 us
  other arithmetic: 15.1 us -> 25.4 us
  starting transfers between devices: 11.7 us -> 7.44 us
    all_gather x0 -> x1, waiting for transfers between devices: none -> 142 us  [shards(): lax.all_gather(placed.astype(jnp.bfloat16), 'fsdp')]
    psum x1 -> x0, waiting for transfers between devices: 77.6 us -> none  [shards(): values_grad = lax.psum(placed.astype(jnp.bfloat16), 'fsdp')]
    reduce_sum x0 -> x1, other arithmetic: none -> 5.24 us  [shards(): jnp.sum(lax.all_gather(placed.astype(jnp.bfloat16), 'fsdp'), axis=0)]
    all_gather x1, waiting for transfers between devices: 28.8 us -> 24.3 us  [shards(): all_keys = lax.all_gather(key_vectors, 'fsdp', axis=0, tiled=True)]
    all_to_all x1, starting transfers between devices: 7.42 us -> 3.57 us  [shards(): lax.all_to_all(attn_inputs, 'fsdp', split_axis=1, concat_axis=0, tiled=True)]
    unnamed x27 -> x15, local copies, waits for them, and re-layouts: 6.41 us -> 4.3 us
  transfers between devices with their start and end apart: 5 -> 5, of which waited for: 3 -> 3; matrix products, arithmetic and copies ran while one was open for 19% -> 13% of each run, Pallas kernels for 0% -> 0%
where the time goes in v1:
time: 271 us; the launch traced here: 270 us
  waiting for transfers between devices  191 us (70%)
  other arithmetic  25.4 us (9%)
  local copies, waits for them, and re-layouts  14.3 us (5%)
  between operations  14.2 us (5%)
  matrix products  10.6 us (4%)
  starting transfers between devices  7.44 us (3%)
  blocking collectives  7.28 us (3%)
    all_gather x1, waiting for transfers between devices, shards(): lax.all_gather(placed.astype(jnp.bfloat16), 'fsdp')  142 us
    all_gather x1, waiting for transfers between devices, shards(): all_keys = lax.all_gather(key_vectors, 'fsdp', axis=0, tiled=True)  24.3 us
    reduce_scatter x1, waiting for transfers between devices, shards(): lax.psum_scatter(weight_grad.astype(jnp.bfloat16), 'side', scatter_dimens...  23.9 us
    select_n x1, other arithmetic, coefficient(): return jnp.where(active, -adv_tok * ratio_now * len_weight, 0.0)  10.8 us
    all_gather x1, blocking collectives, shards(): new_proj = lax.all_gather(new_rows, 'side', axis=0, tiled=True)  7.28 us
  transfers between devices with their start and end apart: 5, of which 3 were waited for; matrix products, arithmetic and copies ran while one was open for 13% of the time, Pallas kernels for 0%

profile of v1, /device:TPU:0, one launch (start us, length us, event | category | flops | bytes accessed | tf_op | source)
XLA Modules:
  0.0 269.8 jit_solution(15094701508646158993)
XLA Ops:
  7.2 0.7 all-gather.3.cloned.1.call-update
  8.0 0.8 convert_reduce_fusion
  8.8 0.7 select_reduce_fusion.2
  9.5 0.7 fusion.36
  10.2 0.8 select_reduce_fusion.1
  11.0 0.7 select_reduce_fusion
  11.7 0.7 fusion.40
  12.4 1.6 fusion.41
  14.0 10.8 %and_select_fusion = f32[128]{0:T(128)S(1)} fusion(f32[128]{0:T(128)} %param.16, f32[128]{0:T(128)} %param.17, s32[]{:T(128)} %bitcast.16, f32[]{:T(128)} %bitcast.7, s32[]{:T(128)} %bitcast.17, f32[]{:T(128)} %bitcast.8, s32[]{:T(128)} %bitcast.18, f32[]{:T(128)} %bitcast.9, s32[]{:T(128)} %bitcast.19, f32[]{:T(128)} %bitcast.10, s32[]{:T(128)} %bitcast.20, ...), kind=kLoop, calls=%fused_computation.78 | loop fusion | flops 6784 | bytes 1608 | tf_op jit(solution)/shard_map/jit(_where)/select_n | solution.py:41
  24.8 1.3 multiply_convert_fusion
  28.8 24.3 %all-gather.3.cloned.1.call-done = bf16[1024,512]{1,0:T(8,128)(2,1)} async-done(((bf16[128,512]{1,0:T(8,128)(2,1)}), bf16[1024,512]{1,0:T(8,128)(2,1)}) %all-gather.3.cloned.1.call-update) | async-done | bytes 1048592 | tf_op jit(solution)/shard_map/all_gather | solution.py:126
  53.1 1.3 fusion.37
  54.5 0.4 fusion.43
  54.8 0.4 fusion.42
  55.2 0.4 fusion.48
  55.6 0.4 fusion.47
  55.9 0.4 fusion.46
  56.3 0.4 fusion.49
  56.6 0.3 fusion.10
  56.9 0.4 convolution_convert_fusion.8
  57.3 0.3 fusion.11
  57.6 0.4 convolution_convert_fusion.7
  58.2 0.4 convolution_convert_fusion.6
  58.9 0.4 convolution_convert_fusion.9
  59.5 0.4 fusion.45
  59.9 0.4 fusion.44
  60.2 0.3 fusion.15
  60.5 0.4 convolution_convert_fusion.3
  60.9 0.3 fusion.16
  61.1 0.4 convolution_convert_fusion.2
  61.8 0.4 convolution_convert_fusion.5
  62.4 0.4 convolution_convert_fusion.4
  63.2 1.1 copy.151
  64.3 0.6 copy-done
  64.9 1.5 copy.153
  66.4 3.6 %all-to-all-start.1 = ((bf16[128,8,640]{0,2,1:T(8,128)(2,1)}), bf16[128,8,640]{0,2,1:T(8,128)(2,1)S(1)}, u32[]{:S(2)}, u32[]{:S(2)}) async-start(bf16[128,8,640]{0,2,1:T(8,128)(2,1)} %bitcast.61), calls=%async_computation.1 | async-start | bytes 2621440 | tf_op jit(solution)/shard_map/all_to_all | solution.py:125
  70.0 141.7 %all-gather.5.cloned.1.call-done = bf16[8,1024,512]{2,1,0:T(8,128)(2,1)} async-done(((bf16[1,1024,512]{2,1,0:T(8,128)(2,1)}), bf16[8,1024,512]{2,1,0:T(8,128)(2,1)}) %all-gather.5.cloned.1.call-update) | async-done | bytes 8388624 | tf_op jit(solution)/shard_map/all_gather | solution.py:145
  211.7 5.2 %reduce_sum.142 = bf16[1024,512]{1,0:T(8,128)(2,1)S(1)} reduce(bf16[8,1024,512]{2,1,0:T(8,128)(2,1)} %all-gather.5.cloned.1.call-done, bf16[]{:T(256)} %constant.80.clone.1), dimensions={0}, to_apply=%region_21.22 | reduce | flops 3670016 | bytes 9437186 | tf_op jit(solution)/shard_map/reduce_sum | solution.py:145
  217.0 2.1 convolution_convert_fusion
  219.0 3.8 %all-to-all-start = ((bf16[8,128,640]{2,1,0:T(8,128)(2,1)}), bf16[8,128,640]{2,1,0:T(8,128)(2,1)S(1)}, u32[]{:S(2)}, u32[]{:S(2)}) async-start(bf16[8,128,640]{2,1,0:T(8,128)(2,1)} %bitcast.127), calls=%async_computation | async-start | bytes 2621440 | tf_op jit(solution)/shard_map/all_to_all | solution.py:149
  222.9 1.5 copy.154
  224.3 2.7 fusion
  227.0 1.1 copy.156
  228.1 23.9 %reduce-scatter.4.cloned.1.call-done = bf16[160,512]{1,0:T(8,128)(2,1)} async-done(((bf16[640,512]{1,0:T(8,128)(2,1)}), bf16[160,512]{1,0:T(8,128)(2,1)}) %reduce-scatter.4.cloned.1.call-update) | async-done | bytes 163856 | tf_op jit(solution)/shard_map/reduce_scatter | solution.py:153
  252.0 1.9 fusion.23
  253.9 7.3 %all_gather.12 = bf16[640,512]{1,0:T(8,128)(2,1)S(1)} all-gather(bf16[160,512]{1,0:T(8,128)(2,1)S(1)} %get-tuple-element.47), channel_id=1, replica_groups=mesh['fsdp'=8,'side'=4] {'side'}, dimensions={0}, use_global_device_ids=true | all-gather | bytes 819200 | tf_op jit(solution)/shard_map/all_gather | solution.py:159
  261.2 1.2 copy.158
  262.5 0.8 copy.168
  (67 shorter events, 4.4 us)
Async XLA Ops:
  7.2 46.0 %all-gather.3.cloned.1.call-start = ((), (), s32[]{:S(2)}) async-start(), calls=%async_computation.3 | async-start | bytes 1179648 | tf_op jit(solution)/shard_map/all_gather | solution.py:126
  7.9 203.8 %all-gather.5.cloned.1.call-start = ((), (), s32[]{:S(2)}) async-start(), calls=%async_computation.4 | async-start | bytes 9437184 | tf_op jit(solution)/shard_map/all_gather | solution.py:145
  26.4 1.1 copy-start.2
  63.2 1.7 copy-start
  66.4 152.6 %all-to-all-start.1 = ((bf16[128,8,640]{0,2,1:T(8,128)(2,1)}), bf16[128,8,640]{0,2,1:T(8,128)(2,1)S(1)}, u32[]{:S(2)}, u32[]{:S(2)}) async-start(bf16[128,8,640]{0,2,1:T(8,128)(2,1)} %bitcast.61), calls=%async_computation.1 | async-start | bytes 2621440 | tf_op jit(solution)/shard_map/all_to_all | solution.py:125
  70.0 147.0 %copy-start.5 = (bf16[640,512]{1,0:T(8,128)(2,1)S(1)}, bf16[640,512]{1,0:T(8,128)(2,1)}, u32[]{:S(2)}) copy-start(bf16[640,512]{1,0:T(8,128)(2,1)} %param.21) | copy-start | bytes 1966084
  217.0 2.1 copy-start.1
  219.0 42.2 %all-to-all-start = ((bf16[8,128,640]{2,1,0:T(8,128)(2,1)}), bf16[8,128,640]{2,1,0:T(8,128)(2,1)S(1)}, u32[]{:S(2)}, u32[]{:S(2)}) async-start(bf16[8,128,640]{2,1,0:T(8,128)(2,1)} %bitcast.127), calls=%async_computation | async-start | bytes 2621440 | tf_op jit(solution)/shard_map/all_to_all | solution.py:149
  222.8 29.2 %reduce-scatter.4.cloned.1.call-start = ((), (), s32[]{:S(2)}) async-start(), calls=%async_computation.5 | async-start | bytes 819200 | tf_op jit(solution)/shard_map/reduce_scatter | solution.py:153
  227.0 25.0 %copy-start.3 = (bf16[160,512]{1,0:T(8,128)(2,1)S(1)}, bf16[160,512]{1,0:T(8,128)(2,1)}, u32[]{:S(2)}) copy-start(bf16[160,512]{1,0:T(8,128)(2,1)} %param.23) | copy-start | bytes 491524
  227.0 25.0 %copy-start.4 = (bf16[160,512]{1,0:T(8,128)(2,1)S(1)}, bf16[160,512]{1,0:T(8,128)(2,1)}, u32[]{:S(2)}) copy-start(bf16[160,512]{1,0:T(8,128)(2,1)} %param.22) | copy-start | bytes 491524
Sparse Core Ops, SparseCore 0:
  10.1 42.9 all-gather.2
  64.4 147.2 all-gather.4
  228.2 23.7 reduce-scatter.3
